TPU v7x, 32 devices: a whole 2x2x4 slice. The times are simulated.
32 devices in a mesh: group: 4 (over y, core), freq: 8 (over z, x).
Axes of the slice: x: 2, y: 2, z: 4, core: 2. Of those that a mesh axis runs over, the one named last changes fastest.
Arguments:
- spectra: bfloat16 [2048, 2, 16], P('freq', None, 'group'), may hold values from -6 to 6
- templates: bfloat16 [2048, 2, 2560], P('freq', None, 'group'), may hold values from -600 to 600
- valid_start: int32 [16], replicated, may hold values from 0 to 2048
Outputs:
- peaks: float32 [2560, 16], P('group')
All inputs are finite; a program needn't handle non-finite values.
Results may differ from a plain program's by a relative error of at most 0.0019.
Values may be sent and summed in bfloat16 or wider, within the bound.
A program may use at most 256 MiB of HBM per device.

v0:
```python
import math
import jax
import jax.numpy as jnp
from jax import lax
from jax.sharding import PartitionSpec as P

N = 4096
VALID = 2048


def make_table(bins_count, lag_index):
    bins_index = jnp.arange(bins_count, dtype=jnp.int32)
    angle = (bins_index[:, None] * lag_index[None, :] % N).astype(jnp.float32) * (2.0 * math.pi / N)
    cosine = jnp.cos(angle)
    sine_part = jnp.sin(angle)
    upper = jnp.concatenate([cosine, sine_part], 1)
    lower = jnp.concatenate([-sine_part, cosine], 1)
    return jnp.concatenate([upper, lower], 0).astype(jnp.bfloat16)


def make_cross(bank_piece, seg_piece):
    bank_re = bank_piece[:, 0, :].astype(jnp.float32)[:, None, :]
    bank_im = bank_piece[:, 1, :].astype(jnp.float32)[:, None, :]
    seg_re = seg_piece[:, 0, :].astype(jnp.float32)[:, :, None]
    seg_im = seg_piece[:, 1, :].astype(jnp.float32)[:, :, None]
    cross_re = bank_re * seg_re + bank_im * seg_im
    cross_im = bank_re * seg_im - bank_im * seg_re
    joined = jnp.stack([cross_re, cross_im], 0).astype(jnp.bfloat16)
    return joined.reshape(2 * joined.shape[1], joined.shape[2] * joined.shape[3])


def contract(cross, table):
    return lax.dot_general(
        cross, table, (((0,), (0,)), ((), ())), preferred_element_type=jnp.float32
    )


def on_device(spectra, templates, valid_start):
    freq_count = lax.axis_size("freq")
    lag_count = N // freq_count
    lag_index = lax.axis_index("freq") * lag_count + jnp.arange(lag_count, dtype=jnp.int32)
    tpl_rows = templates.shape[2]
    every_segment = lax.all_gather(spectra, "group", axis=2, tiled=True)
    count = every_segment.shape[2]
    bank_piece = lax.all_gather(templates, "freq", axis=0, tiled=True)
    seg_piece = lax.all_gather(every_segment, "freq", axis=0, tiled=True)
    width = bank_piece.shape[0]
    cross = make_cross(bank_piece, seg_piece)
    series = contract(cross, make_table(width, lag_index))
    bank_float = bank_piece.astype(jnp.float32)
    norm_sum = jnp.sum(bank_float * bank_float, axis=(0, 1))
    series, template_norm = (series, norm_sum)
    power = (
        series[:, :lag_count] * series[:, :lag_count]
        + series[:, lag_count:] * series[:, lag_count:]
    )
    power = power.reshape(count, tpl_rows, lag_count) / template_norm[None, :, None]
    inside = (lag_index[None, :] >= valid_start[:, None]) & (
        lag_index[None, :] < valid_start[:, None] + VALID
    )
    peaks = jnp.max(jnp.where(inside[:, None, :], power, jnp.float32(0.0)), axis=2).T
    return lax.pmax(peaks, "freq")


def solution(mesh):
    in_specs = (P("freq", None, "group"), P("freq", None, "group"), P())
    out_specs = P("group", None)
    return jax.shard_map(
        on_device, mesh=mesh, in_specs=in_specs, out_specs=out_specs, check_vma=False
    )
```

profile of v0, /device:TPU:0, one launch (start us, length us, event | category | flops | bytes accessed | tf_op | source)
XLA Modules:
  0.0 411.2 jit_solution(10462110616772859024)
XLA Ops:
  6.5 2.0 copy.14
  8.5 0.0 all-gather.2.cloned.1.call-update
  8.6 0.7 copy.15
  9.3 6.3 %all_gather.10 = bf16[256,2,16]{0,1,2:T(2,128)(2,1)S(1)} all-gather(bf16[256,2,4]{0,1,2:T(2,128)(2,1)S(1)} %copy.15), channel_id=1, replica_groups=mesh['group'=4,'freq'=8] {'group'}, dimensions={2}, use_global_device_ids=true | all-gather | bytes 20480 | tf_op jit(solution)/shard_map/all_gather | solution.py:43
  15.5 23.8 %all_gather.11 = bf16[2048,2,16]{0,1,2:T(2,128)(2,1)S(1)} all-gather(bf16[256,2,16]{0,1,2:T(2,128)(2,1)S(1)} %all_gather.10), channel_id=1, replica_groups=mesh['group'=4,'freq'=8] {'freq'}, dimensions={0}, use_global_device_ids=true | all-gather | bytes 147456 | tf_op jit(solution)/shard_map/all_gather | solution.py:46
  39.3 0.2 slice_convert_fusion.1
  39.5 0.3 copy.18
  39.9 0.3 copy.19
  40.2 0.7 broadcast_add_fusion
  40.9 0.7 compare_and_fusion
  41.6 0.2 copy.13
  41.8 2.8 broadcast_in_dim.10
  44.6 5.5 %copy.20 = pred[64,8,16,640]{3,1,2,0:T(8,128)(4,1)} copy(pred[64,8,16,640]{3,2,1,0:T(8,128)(4,1)S(1)} %bitcast.22) | data formatting | bytes 10485760
  50.2 18.7 %fusion.21 = (bf16[2048,512]{1,0:T(8,128)(2,1)}, bf16[2048,512]{1,0:T(8,128)(2,1)}, bf16[2048,512]{1,0:T(8,128)(2,1)}) fusion(s32[512]{0:T(512)S(1)} %iota_add_fusion), kind=kLoop, calls=%fused_computation.34 | loop fusion | flops 18874368 | bytes 6293504 | tf_op jit(solution)/shard_map/convert.9
  68.8 30.4 %all-gather.2.cloned.1.call-done = bf16[2048,2,640]{2,0,1:T(8,128)(2,1)} async-done(((bf16[256,2,640]{2,0,1:T(8,128)(2,1)}), bf16[2048,2,640]{2,0,1:T(8,128)(2,1)}) %all-gather.2.cloned.1.call-update) | async-done | bytes 5242896 | tf_op jit(solution)/shard_map/all_gather | solution.py:45
  99.2 7.2 %fusion.19 = (f32[2048,640]{1,0:T(8,128)}, f32[2048,640]{1,0:T(8,128)}) fusion(bf16[2048,2,640]{2,0,1:T(8,128)(2,1)} %all-gather.2.cloned.1.call-done), kind=kLoop, calls=%fused_computation.32 | loop fusion | flops 2621440 | bytes 15728640 | tf_op jit(solution)/shard_map/mul | solution.py:26
  106.4 31.5 %add_convert_fusion = (bf16[1,2048,16,640]{3,2,1,0:T(8,128)(2,1)}, bf16[1,2048,16,640]{3,2,1,0:T(8,128)(2,1)}) fusion(f32[2048,16]{1,0:T(8,128)S(1)} %bitcast.25, f32[2048,640]{1,0:T(8,128)} %get-tuple-element.8, f32[2048,16]{1,0:T(8,128)S(1)} %bitcast.24, f32[2048,640]{1,0:T(8,128)} %get-tuple-element.7), kind=kLoop, calls=%fused_computation.2 | loop fusion | flops 167772160 | bytes 94633984 | tf_op jit(solution)/shard_map/convert.10
  137.9 56.2 %pad_maximum_fusion = bf16[2,2048,16,640]{3,2,1,0:T(8,128)(2,1)} fusion(bf16[1,2048,16,640]{3,2,1,0:T(8,128)(2,1)} %get-tuple-element.6, bf16[1,2048,16,640]{3,2,1,0:T(8,128)(2,1)} %get-tuple-element.5), kind=kLoop, calls=%fused_computation | loop fusion | flops 41943040 | bytes 167772160 | tf_op jit(solution)/shard_map/stack | solution.py:28
  194.1 55.4 %copy.21 = bf16[512,8,16,640]{3,1,2,0:T(8,128)(2,1)} copy(bf16[512,8,16,640]{3,2,1,0:T(8,128)(2,1)} %bitcast.12) | data formatting | bytes 167772160
  249.5 3.6 multiply_reduce_fusion
  253.1 0.6 div.14
  253.7 99.3 %fusion.4 = f32[10240,1024]{0,1:T(8,128)} fusion(bf16[4096,10240]{1,0:T(8,128)(2,1)} %bitcast.13, bf16[2048,512]{1,0:T(8,128)(2,1)} %get-tuple-element.13, bf16[2048,512]{1,0:T(8,128)(2,1)} %get-tuple-element.12, bf16[2048,512]{1,0:T(8,128)(2,1)S(1)} %copy-done), kind=kOutput, calls=%fused_computation.10 | convolution fusion | flops 85932900352 | bytes 132120576 | tf_op jit(solution)/shard_map/dot_general | solution.py:33
  353.0 15.9 %fusion.3 = f32[10240]{0:T(1024)S(1)} fusion(pred[10240,512]{0,1:T(8,128)(4,1)} %bitcast.23, f32[10240,1024]{0,1:T(8,128)} %fusion.4, f32[10240]{0:T(1024)S(1)} %copy-done.1), kind=kLoop, calls=%fused_computation.8 | loop fusion | flops 31447040 | bytes 47267840 | tf_op jit(solution)/shard_map/reduce_max | solution.py:61
  369.0 35.3 %pmax.7 = f32[640,16]{0,1:T(8,128)} all-reduce(f32[640,16]{0,1:T(8,128)S(1)} %bitcast.26), channel_id=1, replica_groups=mesh['group'=4,'freq'=8] {'freq'}, use_global_device_ids=true, to_apply=%region_2.3 | all-reduce | flops 10240 | bytes 81920 | tf_op jit(solution)/shard_map/pmax | solution.py:62
  (8 shorter events, 0.0 us)
Async XLA Ops:
  6.5 92.7 %all-gather.2.cloned.1.call-start = ((), (), s32[]{:S(2)}) async-start(), calls=%async_computation | async-start | bytes 5898240 | tf_op jit(solution)/shard_map/all_gather | solution.py:45
  194.1 59.7 %copy-start = (bf16[2048,512]{1,0:T(8,128)(2,1)S(1)}, bf16[2048,512]{1,0:T(8,128)(2,1)}, u32[]{:S(2)}) copy-start(bf16[2048,512]{1,0:T(8,128)(2,1)} %get-tuple-element.11) | copy-start | bytes 6291460
  253.7 99.3 %copy-start.1 = (f32[10240]{0:T(1024)S(1)}, f32[10240]{0:T(1024)}, u32[]{:S(2)}) copy-start(f32[10240]{0:T(1024)} %div.14) | copy-start | bytes 122884
Sparse Core Ops, SparseCore 0:
  9.5 89.6 all-gather.1
where the time goes:
time: 411 us
  other arithmetic  135 us (33%)
  matrix products  99.3 us (24%)
  local copies, waits for them, and re-layouts  68 us (17%)
  blocking collectives  65.4 us (16%)
  waiting for transfers between devices  30.4 us (7%)
  between operations  13.5 us (3%)
    dot_general x1, matrix products, contract(): lax.dot_general(cross, table, (((0,), (0,)), ((), ())), preferred_element...  99.3 us
    unnamed x8, local copies, waits for them, and re-layouts  63.7 us
    another operation x1, other arithmetic, make_cross(): joined = jnp.stack([cross_re, cross_im], 0).astype(jnp.bfloat16)  56.2 us
    another operation x2, other arithmetic  50.2 us
    pmax x1, blocking collectives, on_device(): return lax.pmax(peaks, 'freq')  35.3 us
    all_gather x1, waiting for transfers between devices, on_device(): bank_piece = lax.all_gather(templates, 'freq', axis=0, tiled=True)  30.4 us
    all_gather x1, blocking collectives, on_device(): seg_piece = lax.all_gather(every_segment, 'freq', axis=0, tiled=True)  23.8 us
    reduce_max x1, other arithmetic, on_device(): jnp.max(jnp.where(inside[:, None, :], power, jnp.float32(0.0)), axis=2)  15.9 us
  transfers between devices with their start and end apart: 1, of which 1 were waited for; matrix products, arithmetic and copies ran while one was open for 7% of the time, Pallas kernels for 0%

commit v1 on v0

--- a/solution.py
+++ b/solution.py
@@ -3,9 +3,22 @@
 import jax.numpy as jnp
 from jax import lax
 from jax.sharding import PartitionSpec as P
+from jax.lax import axis_index, ppermute, psum
 
 N = 4096
 VALID = 2048
+
+
+def wrap_slices(shard_axis, unit):
+    cores_n = psum(1, axis_name=shard_axis)
+    tile_out = [(pp - 1, pp) for pp in range(1, cores_n)] + [(cores_n - 1, 0)]
+    q_next = unit
+    store = [q_next]
+    for _ in range(cores_n - 1):
+        q_next = ppermute(q_next, axis_name=shard_axis, perm=tile_out)
+        store += [q_next]
+    arr_now = jnp.concatenate([*reversed(store)], 0)
+    return jnp.roll(arr_now, (axis_index(shard_axis) + 1) * q_next.shape[0], 0)
 
 
 def make_table(bins_count, lag_index):
@@ -42,7 +55,7 @@
     tpl_rows = templates.shape[2]
     every_segment = lax.all_gather(spectra, "group", axis=2, tiled=True)
     count = every_segment.shape[2]
-    bank_piece = lax.all_gather(templates, "freq", axis=0, tiled=True)
+    bank_piece = wrap_slices("freq", templates)
     seg_piece = lax.all_gather(every_segment, "freq", axis=0, tiled=True)
     width = bank_piece.shape[0]
     cross = make_cross(bank_piece, seg_piece)

time: 411 us -> 449 us (1.092)
  waiting for transfers between devices: 30.4 us -> 75.2 us
  between operations: 13.5 us -> 0.26 us
  local copies, waits for them, and re-layouts: 68 us -> 75.5 us
  other arithmetic: 135 us -> 130 us
    ppermute x0 -> x7, waiting for transfers between devices: none -> 75.2 us  [wrap_slices(): q_next = ppermute(q_next, axis_name=shard_axis, perm=tile_out)]
    all_gather x1 -> x0, waiting for transfers between devices: 30.4 us -> none  [on_device(): bank_piece = lax.all_gather(templates, 'freq', axis=0, tiled=True)]
    unnamed x8 -> x37, local copies, waits for them, and re-layouts: 63.7 us -> 71 us
  transfers between devices with their start and end apart: 1 -> 7, of which waited for: 1 -> 5; matrix products, arithmetic and copies ran while one was open for 7% -> 7% of each run, Pallas kernels for 0% -> 0%
where the time goes in v1:
time: 449 us
  other arithmetic  130 us (29%)
  matrix products  98.9 us (22%)
  local copies, waits for them, and re-layouts  75.5 us (17%)
  waiting for transfers between devices  75.2 us (17%)
  blocking collectives  65.3 us (15%)
    dot_general x1, matrix products, contract(): lax.dot_general(cross, table, (((0,), (0,)), ((), ())), preferred_element...  98.9 us
    ppermute x7, waiting for transfers between devices, wrap_slices(): q_next = ppermute(q_next, axis_name=shard_axis, perm=tile_out)  75.2 us
    unnamed x37, local copies, waits for them, and re-layouts  71 us
    another operation x1, other arithmetic, make_cross(): joined = jnp.stack([cross_re, cross_im], 0).astype(jnp.bfloat16)  56.2 us
    another operation x2, other arithmetic  50.2 us
    pmax x1, blocking collectives, on_device(): return lax.pmax(peaks, 'freq')  38.4 us
    all_gather x1, blocking collectives, on_device(): seg_piece = lax.all_gather(every_segment, 'freq', axis=0, tiled=True)  21.6 us
    reduce_max x1, other arithmetic, on_device(): jnp.max(jnp.where(inside[:, None, :], power, jnp.float32(0.0)), axis=2)  15.9 us
  transfers between devices with their start and end apart: 7, of which 5 were waited for; matrix products, arithmetic and copies ran while one was open for 7% of the time, Pallas kernels for 0%

profile of v1, /device:TPU:0, one launch (start us, length us, event | category | flops | bytes accessed | tf_op | source)
XLA Modules:
  0.0 449.0 jit_solution(15463776450154694436)
XLA Ops:
  0.0 1.2 copy.18
  1.2 3.0 collective-permute-start
  4.2 17.8 %collective-permute-done = bf16[256,2,640]{2,0,1:T(8,128)(2,1)S(1)} collective-permute-done((bf16[256,2,640]{2,0,1:T(8,128)(2,1)S(1)}, bf16[256,2,640]{2,0,1:T(8,128)(2,1)S(1)}, u32[]{:S(2)}, u32[]{:S(2)}) %collective-permute-start) | collective-permute-done | bytes 655392 | tf_op jit(solution)/shard_map/ppermute | solution.py:18
  22.0 18.6 %collective-permute-done.1 = bf16[256,2,640]{2,0,1:T(8,128)(2,1)S(1)} collective-permute-done((bf16[256,2,640]{2,0,1:T(8,128)(2,1)S(1)}, bf16[256,2,640]{2,0,1:T(8,128)(2,1)S(1)}, u32[]{:S(2)}, u32[]{:S(2)}) %collective-permute-start.1) | collective-permute-done | bytes 655392 | tf_op jit(solution)/shard_map/ppermute | solution.py:18
  41.4 17.7 %collective-permute-done.2 = bf16[256,2,640]{2,0,1:T(8,128)(2,1)S(1)} collective-permute-done((bf16[256,2,640]{2,0,1:T(8,128)(2,1)S(1)}, bf16[256,2,640]{2,0,1:T(8,128)(2,1)S(1)}, u32[]{:S(2)}, u32[]{:S(2)}) %collective-permute-start.2) | collective-permute-done | bytes 655392 | tf_op jit(solution)/shard_map/ppermute | solution.py:18
  60.0 16.9 %collective-permute-done.3 = bf16[256,2,640]{2,0,1:T(8,128)(2,1)S(1)} collective-permute-done((bf16[256,2,640]{2,0,1:T(8,128)(2,1)S(1)}, bf16[256,2,640]{2,0,1:T(8,128)(2,1)S(1)}, u32[]{:S(2)}, u32[]{:S(2)}) %collective-permute-start.3) | collective-permute-done | bytes 655392 | tf_op jit(solution)/shard_map/ppermute | solution.py:18
  78.4 5.2 %all_gather.6 = bf16[256,2,16]{0,1,2:T(2,128)(2,1)S(1)} all-gather(bf16[256,2,4]{0,1,2:T(2,128)(2,1)S(1)} %copy.21), channel_id=1, replica_groups=mesh['group'=4,'freq'=8] {'group'}, dimensions={2}, use_global_device_ids=true | all-gather | bytes 20480 | tf_op jit(solution)/shard_map/all_gather | solution.py:56
  83.6 21.6 %all_gather.7 = bf16[2048,2,16]{0,1,2:T(2,128)(2,1)S(1)} all-gather(bf16[256,2,16]{0,1,2:T(2,128)(2,1)S(1)} %all_gather.6), channel_id=1, replica_groups=mesh['group'=4,'freq'=8] {'freq'}, dimensions={0}, use_global_device_ids=true | all-gather | bytes 147456 | tf_op jit(solution)/shard_map/all_gather | solution.py:59
  105.2 1.2 collective-permute-start.5
  108.9 2.8 broadcast_in_dim.10
  111.7 5.5 %copy.26 = pred[64,8,16,640]{3,1,2,0:T(8,128)(4,1)} copy(pred[64,8,16,640]{3,2,1,0:T(8,128)(4,1)S(1)} %bitcast.22) | data formatting | bytes 10485760
  117.3 4.3 collective-permute-done.5
  121.5 18.7 %fusion.21 = (bf16[2048,512]{1,0:T(8,128)(2,1)}, bf16[2048,512]{1,0:T(8,128)(2,1)}, bf16[2048,512]{1,0:T(8,128)(2,1)}) fusion(s32[512]{0:T(512)S(1)} %iota_add_fusion), kind=kLoop, calls=%fused_computation.34 | loop fusion | flops 18874368 | bytes 6293504 | tf_op jit(solution)/shard_map/convert.9
  140.3 1.2 constant_dynamic-update-slice_fusion.14
  141.5 1.2 constant_dynamic-update-slice_fusion.13
  143.4 1.2 constant_dynamic-update-slice_fusion.6
  144.6 1.2 constant_dynamic-update-slice_fusion.5
  147.4 4.6 %fusion.19 = (f32[2048,640]{1,0:T(8,128)}, f32[2048,640]{1,0:T(8,128)}) fusion(bf16[4096,2,640]{2,0,1:T(8,128)(2,1)S(1)} %constant_dynamic-update-slice_fusion, s32[]{:T(128)S(6)} %select_n.25, s32[]{:T(128)S(6)} %add.55), kind=kLoop, calls=%fused_computation.32 | loop fusion | flops 2621440 | bytes 15728648 | tf_op jit(solution)/shard_map/mul | solution.py:39
  152.1 31.5 %add_convert_fusion = (bf16[1,2048,16,640]{3,2,1,0:T(8,128)(2,1)}, bf16[1,2048,16,640]{3,2,1,0:T(8,128)(2,1)}) fusion(f32[2048,16]{1,0:T(8,128)S(1)} %bitcast.25, f32[2048,640]{1,0:T(8,128)} %get-tuple-element.8, f32[2048,16]{1,0:T(8,128)S(1)} %bitcast.24, f32[2048,640]{1,0:T(8,128)} %get-tuple-element.7), kind=kLoop, calls=%fused_computation.2 | loop fusion | flops 167772160 | bytes 94633984 | tf_op jit(solution)/shard_map/convert.10
  183.5 56.2 %pad_maximum_fusion = bf16[2,2048,16,640]{3,2,1,0:T(8,128)(2,1)} fusion(bf16[1,2048,16,640]{3,2,1,0:T(8,128)(2,1)} %get-tuple-element.6, bf16[1,2048,16,640]{3,2,1,0:T(8,128)(2,1)} %get-tuple-element.5), kind=kLoop, calls=%fused_computation | loop fusion | flops 41943040 | bytes 167772160 | tf_op jit(solution)/shard_map/stack | solution.py:41
  239.7 55.3 %copy.27 = bf16[512,8,16,640]{3,1,2,0:T(8,128)(2,1)} copy(bf16[512,8,16,640]{3,2,1,0:T(8,128)(2,1)} %bitcast.12) | data formatting | bytes 167772160
  295.7 98.9 %fusion.4 = f32[10240,1024]{0,1:T(8,128)} fusion(bf16[4096,10240]{1,0:T(8,128)(2,1)} %bitcast.13, bf16[2048,512]{1,0:T(8,128)(2,1)} %get-tuple-element.13, bf16[2048,512]{1,0:T(8,128)(2,1)} %get-tuple-element.12, bf16[2048,512]{1,0:T(8,128)(2,1)S(1)} %copy-done.7), kind=kOutput, calls=%fused_computation.10 | convolution fusion | flops 85932900352 | bytes 132120576 | tf_op jit(solution)/shard_map/dot_general | solution.py:46
  394.6 15.9 %fusion.3 = f32[10240]{0:T(1024)S(1)} fusion(pred[10240,512]{0,1:T(8,128)(4,1)} %bitcast.23, f32[10240,1024]{0,1:T(8,128)} %fusion.4, f32[10240]{0:T(1024)S(1)} %copy-done.8), kind=kLoop, calls=%fused_computation.8 | loop fusion | flops 31447040 | bytes 47267840 | tf_op jit(solution)/shard_map/reduce_max | solution.py:74
  410.6 38.4 %pmax.7 = f32[640,16]{0,1:T(8,128)} all-reduce(f32[640,16]{0,1:T(8,128)S(1)} %bitcast.26), channel_id=1, replica_groups=mesh['group'=4,'freq'=8] {'freq'}, use_global_device_ids=true, to_apply=%region_2.3 | all-reduce | flops 10240 | bytes 81920 | tf_op jit(solution)/shard_map/pmax | solution.py:75
  (49 shorter events, 8.6 us)
Async XLA Ops:
  1.2 20.8 %collective-permute-start = (bf16[256,2,640]{2,0,1:T(8,128)(2,1)S(1)}, bf16[256,2,640]{2,0,1:T(8,128)(2,1)S(1)}, u32[]{:S(2)}, u32[]{:S(2)}) collective-permute-start(bf16[256,2,640]{2,0,1:T(8,128)(2,1)S(1)} %copy.18), channel_id=1, source_target_pairs={{0,1},{1,2},{2,3},{3,4},{4,5},{5,6},{6,7},{7,0},{8,9},{9,10},{10,1... | collective-permute-start | bytes 1966088 | tf_op jit(solution)/shard_map/ppermute | solution.py:18
  22.0 18.6 %collective-permute-start.1 = (bf16[256,2,640]{2,0,1:T(8,128)(2,1)S(1)}, bf16[256,2,640]{2,0,1:T(8,128)(2,1)S(1)}, u32[]{:S(2)}, u32[]{:S(2)}) collective-permute-start(bf16[256,2,640]{2,0,1:T(8,128)(2,1)S(1)} %collective-permute-done), channel_id=1, source_target_pairs={{0,1},{1,2},{2,3},{3,4},{4,5},{5,6},{6,7},{7,0},{8,9},{9,10},{10,1... | collective-permute-start | bytes 1966088 | tf_op jit(solution)/shard_map/ppermute | solution.py:18
  40.5 0.8 copy-start.1
  41.4 17.7 %collective-permute-start.2 = (bf16[256,2,640]{2,0,1:T(8,128)(2,1)S(1)}, bf16[256,2,640]{2,0,1:T(8,128)(2,1)S(1)}, u32[]{:S(2)}, u32[]{:S(2)}) collective-permute-start(bf16[256,2,640]{2,0,1:T(8,128)(2,1)S(1)} %collective-permute-done.1), channel_id=1, source_target_pairs={{0,1},{1,2},{2,3},{3,4},{4,5},{5,6},{6,7},{7,0},{8,9},{9,10},{10,1... | collective-permute-start | bytes 1966088 | tf_op jit(solution)/shard_map/ppermute | solution.py:18
  59.1 0.8 copy-start.3
  60.0 16.9 %collective-permute-start.3 = (bf16[256,2,640]{2,0,1:T(8,128)(2,1)S(1)}, bf16[256,2,640]{2,0,1:T(8,128)(2,1)S(1)}, u32[]{:S(2)}, u32[]{:S(2)}) collective-permute-start(bf16[256,2,640]{2,0,1:T(8,128)(2,1)S(1)} %collective-permute-done.2), channel_id=1, source_target_pairs={{0,1},{1,2},{2,3},{3,4},{4,5},{5,6},{6,7},{7,0},{8,9},{9,10},{10,1... | collective-permute-start | bytes 1966088 | tf_op jit(solution)/shard_map/ppermute | solution.py:18
  76.9 0.8 copy-start.5
  77.7 27.5 %collective-permute-start.4 = (bf16[256,2,640]{2,0,1:T(8,128)(2,1)S(1)}, bf16[256,2,640]{2,0,1:T(8,128)(2,1)}, u32[]{:S(2)}, u32[]{:S(2)}) collective-permute-start(bf16[256,2,640]{2,0,1:T(8,128)(2,1)S(1)} %collective-permute-done.3), channel_id=1, source_target_pairs={{0,1},{1,2},{2,3},{3,4},{4,5},{5,6},{6,7},{7,0},{8,9},{9,10},{10,1... | collective-permute-start | bytes 1966088 | tf_op jit(solution)/shard_map/ppermute | solution.py:18
  105.2 16.3 %collective-permute-start.5 = (bf16[256,2,640]{2,0,1:T(8,128)(2,1)}, bf16[256,2,640]{2,0,1:T(8,128)(2,1)}, u32[]{:S(2)}, u32[]{:S(2)}) collective-permute-start(bf16[256,2,640]{2,0,1:T(8,128)(2,1)} %collective-permute-done.4), channel_id=1, source_target_pairs={{0,1},{1,2},{2,3},{3,4},{4,5},{5,6},{6,7},{7,0},{8,9},{9,10},{10,1... | collective-permute-start | bytes 1966088 | tf_op jit(solution)/shard_map/ppermute | solution.py:18
  111.7 31.5 %copy-start = (bf16[256,2,640]{2,1,0:T(2,128)(2,1)S(1)}, bf16[256,2,640]{2,1,0:T(2,128)(2,1)}, u32[]{:S(2)}) copy-start(bf16[256,2,640]{2,1,0:T(2,128)(2,1)} %param.4) | copy-start | bytes 1966084
  117.2 25.5 %copy-start.6 = (bf16[256,2,640]{2,0,1:T(8,128)(2,1)S(1)}, bf16[256,2,640]{2,0,1:T(8,128)(2,1)}, u32[]{:S(2)}) copy-start(bf16[256,2,640]{2,0,1:T(8,128)(2,1)} %copy-done.5) | copy-start | bytes 1966084
  117.2 25.6 %copy-start.4 = (bf16[256,2,640]{2,0,1:T(8,128)(2,1)S(1)}, bf16[256,2,640]{2,0,1:T(8,128)(2,1)}, u32[]{:S(2)}) copy-start(bf16[256,2,640]{2,0,1:T(8,128)(2,1)} %copy-done.3) | copy-start | bytes 1966084
  117.2 25.7 %copy-start.2 = (bf16[256,2,640]{2,0,1:T(8,128)(2,1)S(1)}, bf16[256,2,640]{2,0,1:T(8,128)(2,1)}, u32[]{:S(2)}) copy-start(bf16[256,2,640]{2,0,1:T(8,128)(2,1)} %copy-done.1) | copy-start | bytes 1966084
  121.5 18.8 %collective-permute-start.6 = (bf16[256,2,640]{2,0,1:T(8,128)(2,1)}, bf16[256,2,640]{2,0,1:T(8,128)(2,1)S(1)}, u32[]{:S(2)}, u32[]{:S(2)}) collective-permute-start(bf16[256,2,640]{2,0,1:T(8,128)(2,1)} %collective-permute-done.5), channel_id=1, source_target_pairs={{0,1},{1,2},{2,3},{3,4},{4,5},{5,6},{6,7},{7,0},{8,9},{9,10},{10,1... | collective-permute-start | bytes 1966088 | tf_op jit(solution)/shard_map/ppermute | solution.py:18
  239.7 56.0 %copy-start.7 = (bf16[2048,512]{1,0:T(8,128)(2,1)S(1)}, bf16[2048,512]{1,0:T(8,128)(2,1)}, u32[]{:S(2)}) copy-start(bf16[2048,512]{1,0:T(8,128)(2,1)} %get-tuple-element.11) | copy-start | bytes 6291460
  295.7 98.9 %copy-start.8 = (f32[10240]{0:T(1024)S(1)}, f32[10240]{0:T(1024)}, u32[]{:S(2)}) copy-start(f32[10240]{0:T(1024)} %div.14) | copy-start | bytes 122884
